TPU v7x, 128 devices: a whole 4x4x4 slice. The times are simulated.
128 devices in a mesh: batch: 2 (over z_lo), seq: 64 (over y, z_hi, x, core).
Axes of the slice: x: 4, y: 4, z: 4 (z_hi: 2, z_lo: 2; z = z_hi * 2 + z_lo), core: 2. Of those that a mesh axis runs over, the one named last changes fastest.
Arguments:
- query_gate: float32 [4, 16384, 128], P('batch', 'seq'), may hold values from -6 to 6
- key_gate: float32 [4, 16384, 128], P('batch', 'seq'), may hold values from -6 to 6
- value_input: float32 [4, 16384, 128], P('batch', 'seq'), may hold values from -6 to 6
- filters: float32 [128, 16384], P('seq'), may hold values from -1 to 1, as said below
- skip_gain: float32 [128], replicated, may hold values from 0.5 to 1.5
- cotangent: float32 [4, 16384, 128], P('batch', 'seq'), may hold values from -6 to 6
Outputs:
- output: float32 [4, 16384, 128], P('batch', 'seq')
- query_grad: float32 [4, 16384, 128], P('batch', 'seq')
- key_grad: float32 [4, 16384, 128], P('batch', 'seq')
- value_grad: float32 [4, 16384, 128], P('batch', 'seq')
- filter_grad: float32 [128, 16384], P('seq', 'batch')
Inputs may be any that keep to these rules, and one draw needn't show every extreme that they name: `filters`: each channel's filter has a sum of squares of one.
All inputs are finite; a program needn't handle non-finite values.
Results may differ from a plain program's by a relative error of at most 0.0001.
Values sent between devices are 32-bit elements; how exact they have to be, the bound alone decides.
A program may use at most 128 MiB of HBM per device.

v0:
```python
import functools

import jax
import jax.numpy as jnp
import numpy as np
from jax import lax
from jax.experimental import pallas as pl
from jax.experimental.pallas import tpu as pltpu
from jax.sharding import PartitionSpec as P

MESH = pl.DeviceIdType.MESH
F32 = jnp.float32
BF16 = jnp.bfloat16

PEERS = 64
ROWS = 8
K1 = 128
K2 = 256
FULL = K1 * K2


def split_np(table):
    hi = table.astype(BF16)
    lo = (table - hi.astype(np.float64)).astype(BF16)
    return hi, lo


def make_tables():
    k1 = np.arange(K1)
    n1 = np.arange(PEERS)
    n2 = np.arange(K2)
    ang1 = 2.0 * np.pi * (np.outer(k1, n1) % K1) / K1
    c1, s1 = np.cos(ang1), np.sin(ang1)
    left = np.block([[c1, s1], [-s1, c1]])
    left_hi, left_lo = split_np(left)
    left_a = np.concatenate([left_hi, left_hi], axis=1)
    left_f = np.concatenate(
        [left_hi[:, :PEERS], left_hi[:, :PEERS], left_lo[:, :PEERS]], axis=1
    )
    inv_hi, inv_lo = split_np(left.T / FULL)
    inv = np.concatenate([inv_hi, inv_lo], axis=0)
    ang2 = 2.0 * np.pi * (np.outer(n2, n2) % K2) / K2
    c2, s2 = np.cos(ang2), np.sin(ang2)
    right_hi, right_lo = split_np(np.block([[c2, -s2], [s2, c2]]))
    angt = 2.0 * np.pi * (np.outer(k1, n2) % FULL) / FULL
    twist = np.concatenate([np.cos(angt), np.sin(angt)], axis=0).astype(np.float32)
    return (left_a, left_lo, left_f, inv, right_hi, right_lo, twist)


def halves(x):
    hi = x.astype(BF16)
    lo = (x - hi.astype(F32)).astype(BF16)
    return hi, lo


def dot(a, b):
    return jnp.dot(a, b, preferred_element_type=F32)


def turn_forward(section, twist):
    re, im = section[:K1], section[K1:]
    tc, ts = twist[:K1], twist[K1:]
    return re * tc + im * ts, im * tc - re * ts


def turn_inverse(re, im, twist):
    tc, ts = twist[:K1], twist[K1:]
    return re * tc - im * ts, im * tc + re * ts


def put_pair(pair_ref, channel, first, second):
    for part, value in enumerate((first, second)):
        hi, lo = halves(value)
        pair_ref[channel * K1 : (channel + 1) * K1, part * K2 : (part + 1) * K2] = hi
        pair_ref[
            2 * K1 + channel * K1 : 2 * K1 + (channel + 1) * K1, part * K2 : (part + 1) * K2
        ] = lo


def second_stage(pair_ref, right_hi, right_lo):
    wide = dot(pair_ref[...], right_hi[...])
    return wide[: 2 * K1] + wide[2 * K1 :] + dot(pair_ref[: 2 * K1, :], right_lo[...])


def gather_rows(block_ref, row):
    return block_ref[pl.ds(row, PEERS, stride=ROWS), :]


def forward(block_ref, spec_ref, pair_ref, tables):
    left_a, left_lo, _, _, right_hi, right_lo, twist = tables
    for c in range(2):
        rows = [
            jnp.concatenate(
                [gather_rows(block_ref, c * 4 + b * 2), gather_rows(block_ref, c * 4 + b * 2 + 1)],
                axis=1,
            )
            for b in range(2)
        ]
        hi, lo = halves(jnp.concatenate(rows, axis=0))
        section = dot(left_a[...], jnp.concatenate([hi, lo], axis=0)) + dot(left_lo[...], hi)
        put_pair(pair_ref, c, *turn_forward(section, twist))
    spec_ref[...] = second_stage(pair_ref, right_hi, right_lo)


def forward_filters(rows_ref, spec_ref, pair_ref, tables):
    _, _, left_f, _, right_hi, right_lo, twist = tables
    for c in range(2):
        hi, lo = halves(rows_ref[c * PEERS : (c + 1) * PEERS, :])
        section = dot(left_f[...], jnp.concatenate([hi, lo, hi], axis=0))
        put_pair(pair_ref, c, *turn_forward(section, twist))
    spec_ref[...] = second_stage(pair_ref, right_hi, right_lo)


def multiply(left_ref, right_ref, c, conjugate_left):
    rows = slice(c * K1, (c + 1) * K1)
    lr, li = left_ref[rows, :K2], left_ref[rows, K2:]
    rr, ri = right_ref[rows, :K2], right_ref[rows, K2:]
    if conjugate_left:
        return lr * rr + li * ri, lr * ri - li * rr
    return lr * rr - li * ri, lr * ri + li * rr


def inverse(left_ref, right_ref, conjugate_left, pair_ref, wide_ref, tables, real_only):
    _, _, _, inv, right_hi, right_lo, twist = tables
    for c in range(2):
        re, im = multiply(left_ref, right_ref, c, conjugate_left)
        put_pair(pair_ref, c, im, re)
    wide_ref[...] = second_stage(pair_ref, right_hi, right_lo)
    results = []
    for c in range(2):
        rows = slice(c * K1, (c + 1) * K1)
        re, im = turn_inverse(wide_ref[rows, K2:], wide_ref[rows, :K2], twist)
        hi, lo = halves(jnp.concatenate([re, im], axis=0))
        if real_only:
            results.append(
                dot(inv[:PEERS, :], hi) + dot(inv[2 * PEERS : 3 * PEERS, :], hi) + dot(inv[:PEERS, :], lo)
            )
        else:
            both = dot(inv[...], hi)
            results.append(both[:K1] + both[K1:] + dot(inv[:K1, :], lo))
    return results


def main_kernel(
    query_hbm, key_hbm, value_hbm, cotangent_hbm, filters_hbm, *rest
):
    table_hbm, rest = rest[:7], rest[7:]
    conv_out, back_out, lag_own_out, lag_other_out = rest[:4]
    rest = rest[4:]
    query, key, value, cotangent, filters = rest[:5]
    tables, rest = rest[5:12], rest[12:]
    (
        mixed_send, up_send, mixed_got, up_got, conv_send, back_send,
        filter_rows, filter_spec, mixed_spec, up_spec, pair, wide, lag, lag_got,
        load_sem, send_sem, recv_sem, lag_sem, own_sem,
    ) = rest
    b = lax.axis_index("batch")
    s = lax.axis_index("seq")

    loads = [
        pltpu.make_async_copy(src, dst, load_sem.at[i])
        for i, (src, dst) in enumerate(
            zip(
                (key_hbm, value_hbm, query_hbm, cotangent_hbm, filters_hbm) + tuple(table_hbm),
                (key, value, query, cotangent, filters) + tuple(tables),
            )
        )
    ]
    for load in loads:
        load.start()

    def peer(i):
        turn = lax.rem(i - 1 + s * 17, PEERS - 1) + 1
        return lax.rem(s + turn * 23, PEERS)

    barrier = pltpu.get_barrier_semaphore()

    def greet(i, carry):
        pl.semaphore_signal(barrier, inc=1, device_id=(b, peer(i)), device_id_type=MESH)
        return carry

    lax.fori_loop(1, PEERS, greet, 0)
    pl.semaphore_signal(barrier, inc=1, device_id=(1 - b, s), device_id_type=MESH)

    for first, second, left, right, target in (
        (0, 1, key, value, mixed_send),
        (2, 3, query, cotangent, up_send),
    ):
        loads[first].wait()
        loads[second].wait()
        for bb in range(2):
            for half in range(2):
                tokens = slice(half * 128, (half + 1) * 128)
                product = left[bb, tokens, :] * right[bb, tokens, :]
                target[pl.ds(bb * 2 + half, 128, stride=4), :] = product.T

    pl.semaphore_wait(barrier, PEERS)

    def block(i):
        return pl.ds(pl.multiple_of(i * ROWS, ROWS), ROWS)

    def send(source, target, k):
        def one(i, carry):
            d = peer(i)
            pltpu.make_async_remote_copy(
                src_ref=source.at[block(d)],
                dst_ref=target.at[block(s)],
                send_sem=send_sem.at[k],
                recv_sem=recv_sem.at[k],
                device_id=(b, d),
                device_id_type=MESH,
            ).start()
            return carry

        lax.fori_loop(1, PEERS, one, 0)

    def settled(source, target, k):
        rows = pl.ds(0, (PEERS - 1) * ROWS)
        return pltpu.make_async_remote_copy(
            src_ref=source.at[rows],
            dst_ref=target.at[rows],
            send_sem=send_sem.at[k],
            recv_sem=recv_sem.at[k],
            device_id=(1 - b, s),
            device_id_type=MESH,
        )

    send(mixed_send, mixed_got, 0)
    send(up_send, up_got, 1)
    mixed_got[block(s), :] = mixed_send[block(s), :]
    up_got[block(s), :] = up_send[block(s), :]

    for load in loads[4:]:
        load.wait()
    for c in range(2):
        for n1 in range(PEERS):
            filter_rows[c * PEERS + n1 : c * PEERS + n1 + 1, :] = filters[
                c : c + 1, n1 * K2 : (n1 + 1) * K2
            ]
    forward_filters(filter_rows, filter_spec, pair, tables)

    def spread(results, target):
        for c in range(2):
            for bb in range(2):
                for half in range(2):
                    target[pl.ds(c * 4 + bb * 2 + half, PEERS, stride=ROWS), :] = results[c][
                        bb * PEERS : (bb + 1) * PEERS, half * 128 : (half + 1) * 128
                    ]

    settled(mixed_send, mixed_got, 0).wait_recv()
    forward(mixed_got, mixed_spec, pair, tables)
    spread(inverse(mixed_spec, filter_spec, False, pair, wide, tables, False), conv_send)
    send(conv_send, conv_out, 2)
    own_conv = pltpu.make_async_copy(conv_send.at[block(s)], conv_out.at[block(s)], own_sem.at[0])
    own_conv.start()

    settled(up_send, up_got, 1).wait_recv()
    forward(up_got, up_spec, pair, tables)
    spread(inverse(filter_spec, up_spec, True, pair, wide, tables, False), back_send)
    send(back_send, back_out, 3)
    own_back = pltpu.make_async_copy(back_send.at[block(s)], back_out.at[block(s)], own_sem.at[1])
    own_back.start()

    results = inverse(mixed_spec, up_spec, True, pair, wide, tables, True)
    for half in range(2):
        for c in range(2):
            lag[half, c * 32 : (c + 1) * 32, :] = results[c][half * 32 : (half + 1) * 32, :]
    lag_copy = pltpu.make_async_remote_copy(
        src_ref=lag.at[1 - b],
        dst_ref=lag_got,
        send_sem=lag_sem.at[0],
        recv_sem=lag_sem.at[1],
        device_id=(1 - b, s),
        device_id_type=MESH,
    )
    lag_copy.start()
    own_lag = pltpu.make_async_copy(lag.at[b], lag_own_out, own_sem.at[2])
    own_lag.start()
    lag_copy.wait_recv()
    other_lag = pltpu.make_async_copy(lag_got, lag_other_out, own_sem.at[3])
    other_lag.start()

    settled(mixed_send, mixed_got, 0).wait_send()
    settled(up_send, up_got, 1).wait_send()
    settled(conv_send, conv_out, 2).wait()
    settled(back_send, back_out, 3).wait()
    lag_copy.wait_send()
    own_conv.wait()
    own_back.wait()
    own_lag.wait()
    other_lag.wait()


def final_kernel(
    conv, back, lag_own, lag_other, query, key, value, cotangent, skip,
    output, query_grad, key_grad, value_grad, filter_grad,
):
    gain = skip[...]
    for bb in range(2):
        for half in range(2):
            tokens = slice(half * 128, (half + 1) * 128)
            q, k = query[bb, tokens, :], key[bb, tokens, :]
            v, g = value[bb, tokens, :], cotangent[bb, tokens, :]
            rows = pl.ds(bb * 2 + half, 128, stride=4)
            hidden = conv[rows, :].T + gain * (k * v)
            output[bb, tokens, :] = q * hidden
            query_grad[bb, tokens, :] = g * hidden
            mixed_grad = back[rows, :].T + gain * (g * q)
            key_grad[bb, tokens, :] = mixed_grad * v
            value_grad[bb, tokens, :] = mixed_grad * k
    total = (lag_own[...] + lag_other[...]) * (1.0 / 128.0)
    for c in range(2):
        for n in range(32):
            filter_grad[c : c + 1, n * K2 : (n + 1) * K2] = total[c * 32 + n : c * 32 + n + 1, :]


def per_device(query, key, value, filters, skip, cotangent):
    tables = [jnp.asarray(t) for t in make_tables()]
    message = (PEERS * ROWS, 128)
    any_space = pl.BlockSpec(memory_space=pl.ANY)
    in_vmem = pl.BlockSpec(memory_space=pltpu.VMEM)
    vmem = pltpu.VMEM
    tokens = query.shape
    conv, back, lag_own, lag_other = pl.pallas_call(
        main_kernel,
        out_shape=(
            jax.ShapeDtypeStruct(message, F32),
            jax.ShapeDtypeStruct(message, F32),
            jax.ShapeDtypeStruct((64, K2), F32),
            jax.ShapeDtypeStruct((64, K2), F32),
        ),
        in_specs=[any_space] * 12,
        out_specs=(any_space,) * 4,
        scratch_shapes=[vmem(tokens, F32)] * 4
        + [vmem(filters.shape, F32)]
        + [vmem(t.shape, t.dtype) for t in tables]
        + [vmem(message, F32)] * 6
        + [vmem((2 * PEERS, K2), F32)]
        + [vmem((2 * K1, 2 * K2), F32)] * 3
        + [vmem((4 * K1, 2 * K2), BF16), vmem((2 * K1, 2 * K2), F32)]
        + [vmem((2, 64, K2), F32), vmem((64, K2), F32)]
        + [
            pltpu.SemaphoreType.DMA((12,)),
            pltpu.SemaphoreType.DMA((4,)),
            pltpu.SemaphoreType.DMA((4,)),
            pltpu.SemaphoreType.DMA((2,)),
            pltpu.SemaphoreType.DMA((4,)),
        ],
        compiler_params=pltpu.CompilerParams(
            collective_id=0, has_side_effects=True, vmem_limit_bytes=40 * 1024 * 1024
        ),
        name="spectral_exchange",
    )(query, key, value, cotangent, filters, *tables)
    block = jax.ShapeDtypeStruct(tokens, F32)
    return pl.pallas_call(
        final_kernel,
        out_shape=(block, block, block, block, jax.ShapeDtypeStruct((2, 32 * K2), F32)),
        in_specs=[in_vmem] * 9,
        out_specs=(in_vmem,) * 5,
        name="gates",
    )(conv, back, lag_own, lag_other, query, key, value, cotangent, skip.reshape(1, -1))


def solution(mesh):
    rows = P("batch", "seq", None)
    return jax.shard_map(
        per_device,
        mesh=mesh,
        in_specs=(rows, rows, rows, P("seq", None), P(), rows),
        out_specs=(rows, rows, rows, rows, P("seq", "batch")),
        check_vma=False,
    )
```

profile of v0, /device:TPU:1, one launch (start us, length us, event | category | flops | bytes accessed | tf_op | source)
XLA Modules:
  0.0 49.2 jit_solution(10070683574136225609)
XLA Ops:
  0.6 0.0 copy-start
  0.6 0.9 %copy-done = f32[2,256,128]{2,1,0:T(8,128)S(1)} copy-done((f32[2,256,128]{2,1,0:T(8,128)S(1)}, f32[2,256,128]{2,1,0:T(8,128)}, u32[]{:S(2)}) %copy-start) | copy-done | bytes 262168
  1.6 0.0 copy-start.1
  1.6 0.9 %copy-done.1 = f32[2,256,128]{2,1,0:T(8,128)S(1)} copy-done((f32[2,256,128]{2,1,0:T(8,128)S(1)}, f32[2,256,128]{2,1,0:T(8,128)}, u32[]{:S(2)}) %copy-start.1) | copy-done | bytes 262168
  2.5 0.0 copy-start.2
  2.5 0.9 %copy-done.2 = f32[2,256,128]{2,1,0:T(8,128)S(1)} copy-done((f32[2,256,128]{2,1,0:T(8,128)S(1)}, f32[2,256,128]{2,1,0:T(8,128)}, u32[]{:S(2)}) %copy-start.2) | copy-done | bytes 262168
  3.5 0.0 copy-start.3
  3.5 0.9 %copy-done.3 = f32[2,256,128]{2,1,0:T(8,128)S(1)} copy-done((f32[2,256,128]{2,1,0:T(8,128)S(1)}, f32[2,256,128]{2,1,0:T(8,128)}, u32[]{:S(2)}) %copy-start.3) | copy-done | bytes 262168
  4.4 0.0 copy-start.4
  4.4 1.0 %copy-done.4 = bf16[512,512]{1,0:T(8,128)(2,1)S(1)} copy-done((bf16[512,512]{1,0:T(8,128)(2,1)S(1)}, bf16[512,512]{1,0:T(8,128)(2,1)}, u32[]{:S(2)}) %copy-start.4) | copy-done | bytes 524312
  5.5 1.0 %copy-done.5 = bf16[512,512]{1,0:T(8,128)(2,1)S(1)} copy-done((bf16[512,512]{1,0:T(8,128)(2,1)S(1)}, bf16[512,512]{1,0:T(8,128)(2,1)}, u32[]{:S(2)}) %copy-start.5) | copy-done | bytes 524312
  6.5 0.9 %copy-done.6 = f32[256,256]{1,0:T(8,128)S(1)} copy-done((f32[256,256]{1,0:T(8,128)S(1)}, f32[256,256]{1,0:T(8,128)}, u32[]{:S(2)}) %copy-start.6) | copy-done | bytes 262168
  7.5 0.9 %copy-done.9 = f32[2,16384]{1,0:T(2,128)S(1)} copy-done((f32[2,16384]{1,0:T(2,128)S(1)}, f32[2,16384]{1,0:T(2,128)}, u32[]{:S(2)}) %copy-start.9) | copy-done | bytes 131096
  8.4 0.9 %copy-done.10 = bf16[256,256]{1,0:T(8,128)(2,1)S(1)} copy-done((bf16[256,256]{1,0:T(8,128)(2,1)S(1)}, bf16[256,256]{1,0:T(8,128)(2,1)}, u32[]{:S(2)}) %copy-start.10) | copy-done | bytes 131096
  9.3 0.9 %copy-done.11 = bf16[256,192]{1,0:T(8,128)(2,1)S(1)} copy-done((bf16[256,192]{1,0:T(8,128)(2,1)S(1)}, bf16[256,192]{1,0:T(8,128)(2,1)}, u32[]{:S(2)}) %copy-start.11) | copy-done | bytes 98328
  10.2 0.9 %copy-done.12 = bf16[256,256]{1,0:T(8,128)(2,1)S(1)} copy-done((bf16[256,256]{1,0:T(8,128)(2,1)S(1)}, bf16[256,256]{1,0:T(8,128)(2,1)}, u32[]{:S(2)}) %copy-start.12) | copy-done | bytes 131096
  11.1 0.8 %copy-done.15 = bf16[256,128]{1,0:T(8,128)(2,1)S(1)} copy-done((bf16[256,128]{1,0:T(8,128)(2,1)S(1)}, bf16[256,128]{1,0:T(8,128)(2,1)}, u32[]{:S(2)}) %copy-start.15) | copy-done | bytes 65560
  11.9 32.1 %spectral_exchange.1 = (f32[512,128]{1,0:T(8,128)S(1)}, f32[512,128]{1,0:T(8,128)S(1)}, f32[64,256]{1,0:T(8,128)S(1)}, f32[64,256]{1,0:T(8,128)S(1)}) custom-call(f32[2,256,128]{2,1,0:T(8,128)S(1)} %copy-done, f32[2,256,128]{2,1,0:T(8,128)S(1)} %copy-done.1, f32[2,256,128]{2,1,0:T(8,128)S(1)} %copy-done.2, f32[2,256,128]{2,1,0:T(8,128)S(1)} %copy-done.3, ...), custom_call_target="tpu_custom_call" | custom-call | tf_op jit(solution)/shard_map/spectral_exchange/pallas_call | solution.py:324
  44.0 0.0 copy-start.7
  44.0 0.7 %copy-done.7 = f32[512,128]{1,0:T(8,128)} copy-done((f32[512,128]{1,0:T(8,128)}, f32[512,128]{1,0:T(8,128)S(1)}, u32[]{:S(2)}) %copy-start.7) | copy-done | bytes 262168
  44.7 0.7 %copy-done.8 = f32[512,128]{1,0:T(8,128)} copy-done((f32[512,128]{1,0:T(8,128)}, f32[512,128]{1,0:T(8,128)S(1)}, u32[]{:S(2)}) %copy-start.8) | copy-done | bytes 262168
  45.4 0.6 %copy-done.13 = f32[64,256]{1,0:T(8,128)} copy-done((f32[64,256]{1,0:T(8,128)}, f32[64,256]{1,0:T(8,128)S(1)}, u32[]{:S(2)}) %copy-start.13) | copy-done | bytes 65560
  46.0 0.6 %copy-done.14 = f32[64,256]{1,0:T(8,128)} copy-done((f32[64,256]{1,0:T(8,128)}, f32[64,256]{1,0:T(8,128)S(1)}, u32[]{:S(2)}) %copy-start.14) | copy-done | bytes 65560
  46.7 2.6 %gates.1 = (f32[2,256,128]{2,1,0:T(8,128)}, f32[2,256,128]{2,1,0:T(8,128)}, f32[2,256,128]{2,1,0:T(8,128)}, f32[2,256,128]{2,1,0:T(8,128)}, f32[2,8192]{1,0:T(2,128)}) custom-call(f32[512,128]{1,0:T(8,128)} %copy-done.7, f32[512,128]{1,0:T(8,128)} %copy-done.8, f32[64,256]{1,0:T(8,128)} %copy-done.13, f32[64,256]{1,0:T(8,128)} %copy-done.14, ...), custom_call_target="tpu_custom_call" | custom-call | tf_op jit(solution)/shard_map/gates/pallas_call | solution.py:355
  (10 shorter events, 0.0 us)
Async XLA Ops:
  0.6 1.0 %copy-start = (f32[2,256,128]{2,1,0:T(8,128)S(1)}, f32[2,256,128]{2,1,0:T(8,128)}, u32[]{:S(2)}) copy-start(f32[2,256,128]{2,1,0:T(8,128)} %query.1) | copy-start | bytes 786436
  1.6 0.9 %copy-start.1 = (f32[2,256,128]{2,1,0:T(8,128)S(1)}, f32[2,256,128]{2,1,0:T(8,128)}, u32[]{:S(2)}) copy-start(f32[2,256,128]{2,1,0:T(8,128)} %key.1) | copy-start | bytes 786436
  2.5 0.9 %copy-start.2 = (f32[2,256,128]{2,1,0:T(8,128)S(1)}, f32[2,256,128]{2,1,0:T(8,128)}, u32[]{:S(2)}) copy-start(f32[2,256,128]{2,1,0:T(8,128)} %value.1) | copy-start | bytes 786436
  3.5 0.9 %copy-start.3 = (f32[2,256,128]{2,1,0:T(8,128)S(1)}, f32[2,256,128]{2,1,0:T(8,128)}, u32[]{:S(2)}) copy-start(f32[2,256,128]{2,1,0:T(8,128)} %cotangent.1) | copy-start | bytes 786436
  4.4 1.0 %copy-start.4 = (bf16[512,512]{1,0:T(8,128)(2,1)S(1)}, bf16[512,512]{1,0:T(8,128)(2,1)}, u32[]{:S(2)}) copy-start(bf16[512,512]{1,0:T(8,128)(2,1)} %constant.19.clone.rest_5_) | copy-start | bytes 1572868
  5.5 1.0 %copy-start.5 = (bf16[512,512]{1,0:T(8,128)(2,1)S(1)}, bf16[512,512]{1,0:T(8,128)(2,1)}, u32[]{:S(2)}) copy-start(bf16[512,512]{1,0:T(8,128)(2,1)} %constant.18.clone.rest_4_) | copy-start | bytes 1572868
  6.5 0.9 %copy-start.6 = (f32[256,256]{1,0:T(8,128)S(1)}, f32[256,256]{1,0:T(8,128)}, u32[]{:S(2)}) copy-start(f32[256,256]{1,0:T(8,128)} %constant.20.clone.rest_6_) | copy-start | bytes 786436
  7.5 0.9 %copy-start.9 = (f32[2,16384]{1,0:T(2,128)S(1)}, f32[2,16384]{1,0:T(2,128)}, u32[]{:S(2)}) copy-start(f32[2,16384]{1,0:T(2,128)} %filters_hbm.1) | copy-start | bytes 393220
  8.4 0.9 %copy-start.10 = (bf16[256,256]{1,0:T(8,128)(2,1)S(1)}, bf16[256,256]{1,0:T(8,128)(2,1)}, u32[]{:S(2)}) copy-start(bf16[256,256]{1,0:T(8,128)(2,1)} %constant.17.clone.rest_3_) | copy-start | bytes 393220
  9.3 0.9 %copy-start.11 = (bf16[256,192]{1,0:T(8,128)(2,1)S(1)}, bf16[256,192]{1,0:T(8,128)(2,1)}, u32[]{:S(2)}) copy-start(bf16[256,192]{1,0:T(8,128)(2,1)} %constant.16.clone.rest_2_) | copy-start | bytes 294916
  10.2 0.9 %copy-start.12 = (bf16[256,256]{1,0:T(8,128)(2,1)S(1)}, bf16[256,256]{1,0:T(8,128)(2,1)}, u32[]{:S(2)}) copy-start(bf16[256,256]{1,0:T(8,128)(2,1)} %constant.14.clone.rest_0_) | copy-start | bytes 393220
  11.1 0.8 %copy-start.15 = (bf16[256,128]{1,0:T(8,128)(2,1)S(1)}, bf16[256,128]{1,0:T(8,128)(2,1)}, u32[]{:S(2)}) copy-start(bf16[256,128]{1,0:T(8,128)(2,1)} %constant.15.clone.rest_1_) | copy-start | bytes 196612
  44.0 0.7 %copy-start.7 = (f32[512,128]{1,0:T(8,128)}, f32[512,128]{1,0:T(8,128)S(1)}, u32[]{:S(2)}) copy-start(f32[512,128]{1,0:T(8,128)S(1)} %get-tuple-element.9.conv) | copy-start | bytes 786436
  44.7 0.7 %copy-start.8 = (f32[512,128]{1,0:T(8,128)}, f32[512,128]{1,0:T(8,128)S(1)}, u32[]{:S(2)}) copy-start(f32[512,128]{1,0:T(8,128)S(1)} %get-tuple-element.10.back) | copy-start | bytes 786436
  45.4 0.6 %copy-start.13 = (f32[64,256]{1,0:T(8,128)}, f32[64,256]{1,0:T(8,128)S(1)}, u32[]{:S(2)}) copy-start(f32[64,256]{1,0:T(8,128)S(1)} %get-tuple-element.11.lag_own) | copy-start | bytes 196612
  46.0 0.6 %copy-start.14 = (f32[64,256]{1,0:T(8,128)}, f32[64,256]{1,0:T(8,128)S(1)}, u32[]{:S(2)}) copy-start(f32[64,256]{1,0:T(8,128)S(1)} %get-tuple-element.12.lag_other) | copy-start | bytes 196612
where the time goes:
time: 49.8 us; the launch traced here: 49.2 us
  Pallas kernels  34.7 us (70%)
  local copies, waits for them, and re-layouts  13.9 us (28%)
  between operations  0.67 us (1%)
    pallas_call x1, Pallas kernels, per_device(): pl.pallas_call(main_kernel, out_shape=(jax.ShapeDtypeStruct(message, F32)...  32.1 us
    unnamed x32, local copies, waits for them, and re-layouts  13.9 us
    pallas_call x1, Pallas kernels, per_device(): pl.pallas_call(final_kernel, out_shape=(block, block, block, block, jax.S...  2.59 us

commit v1 on v0

--- a/solution.py
+++ b/solution.py
@@ -293,9 +293,11 @@
 
 def final_kernel(
     conv, back, lag_own, lag_other, query, key, value, cotangent, skip,
-    output, query_grad, key_grad, value_grad, filter_grad,
+    output_hbm, query_grad_hbm, key_grad_hbm, value_grad_hbm, filter_grad_hbm,
+    output, query_grad, key_grad, value_grad, filter_grad, out_sem, lag_sem,
 ):
     gain = skip[...]
+    stores = []
     for bb in range(2):
         for half in range(2):
             tokens = slice(half * 128, (half + 1) * 128)
@@ -303,24 +305,39 @@
             v, g = value[bb, tokens, :], cotangent[bb, tokens, :]
             rows = pl.ds(bb * 2 + half, 128, stride=4)
             hidden = conv[rows, :].T + gain * (k * v)
-            output[bb, tokens, :] = q * hidden
-            query_grad[bb, tokens, :] = g * hidden
             mixed_grad = back[rows, :].T + gain * (g * q)
-            key_grad[bb, tokens, :] = mixed_grad * v
-            value_grad[bb, tokens, :] = mixed_grad * k
+            for i, (result, src, dst) in enumerate(
+                (
+                    (q * hidden, output, output_hbm),
+                    (g * hidden, query_grad, query_grad_hbm),
+                    (mixed_grad * v, key_grad, key_grad_hbm),
+                    (mixed_grad * k, value_grad, value_grad_hbm),
+                )
+            ):
+                src[bb, tokens, :] = result
+                store = pltpu.make_async_copy(
+                    src.at[bb, tokens], dst.at[bb, tokens], out_sem.at[bb * 2 + half, i]
+                )
+                store.start()
+                stores.append(store)
     total = (lag_own[...] + lag_other[...]) * (1.0 / 128.0)
     for c in range(2):
         for n in range(32):
             filter_grad[c : c + 1, n * K2 : (n + 1) * K2] = total[c * 32 + n : c * 32 + n + 1, :]
+    store = pltpu.make_async_copy(filter_grad, filter_grad_hbm, lag_sem)
+    store.start()
+    stores.append(store)
+    for store in stores:
+        store.wait()
 
 
 def per_device(query, key, value, filters, skip, cotangent):
     tables = [jnp.asarray(t) for t in make_tables()]
     message = (PEERS * ROWS, 128)
-    any_space = pl.BlockSpec(memory_space=pl.ANY)
-    in_vmem = pl.BlockSpec(memory_space=pltpu.VMEM)
+    in_hbm = pl.BlockSpec(memory_space=pltpu.HBM)
     vmem = pltpu.VMEM
     tokens = query.shape
+    operands = (query, key, value, cotangent, filters, *tables)
     conv, back, lag_own, lag_other = pl.pallas_call(
         main_kernel,
         out_shape=(
@@ -329,8 +346,8 @@
             jax.ShapeDtypeStruct((64, K2), F32),
             jax.ShapeDtypeStruct((64, K2), F32),
         ),
-        in_specs=[any_space] * 12,
-        out_specs=(any_space,) * 4,
+        in_specs=[in_hbm] * 12,
+        out_specs=(in_hbm,) * 4,
         scratch_shapes=[vmem(tokens, F32)] * 4
         + [vmem(filters.shape, F32)]
         + [vmem(t.shape, t.dtype) for t in tables]
@@ -350,13 +367,16 @@
             collective_id=0, has_side_effects=True, vmem_limit_bytes=40 * 1024 * 1024
         ),
         name="spectral_exchange",
-    )(query, key, value, cotangent, filters, *tables)
+    )(*[pltpu.with_memory_space_constraint(x, pltpu.HBM) for x in operands])
     block = jax.ShapeDtypeStruct(tokens, F32)
     return pl.pallas_call(
         final_kernel,
         out_shape=(block, block, block, block, jax.ShapeDtypeStruct((2, 32 * K2), F32)),
-        in_specs=[in_vmem] * 9,
-        out_specs=(in_vmem,) * 5,
+        in_specs=[pl.BlockSpec(memory_space=pltpu.VMEM)] * 9,
+        out_specs=(in_hbm,) * 5,
+        scratch_shapes=[vmem(tokens, F32)] * 4
+        + [vmem((2, 32 * K2), F32), pltpu.SemaphoreType.DMA((4, 4)), pltpu.SemaphoreType.DMA],
+        compiler_params=pltpu.CompilerParams(vmem_limit_bytes=40 * 1024 * 1024),
         name="gates",
     )(conv, back, lag_own, lag_other, query, key, value, cotangent, skip.reshape(1, -1))
 

time: 49.8 us -> 34 us (0.68)
  local copies, waits for them, and re-layouts: 13.9 us -> 0.63 us
  Pallas kernels: 34.7 us -> 32.5 us
    unnamed x32 -> x10, local copies, waits for them, and re-layouts: 13.9 us -> 0.63 us
    pallas_call x1, Pallas kernels: 2.59 us -> 1.22 us  [per_device(): pl.pallas_call(final_kernel, out_shape=(block, block, block, block, jax.S...]
    pallas_call x1, Pallas kernels: 32.1 us -> 31.3 us  [per_device(): pl.pallas_call(main_kernel, out_shape=(jax.ShapeDtypeStruct(message, F32)...]
where the time goes in v1:
time: 34 us; the launch traced here: 33.9 us
  Pallas kernels  32.5 us (96%)
  between operations  0.71 us (2%)
  local copies, waits for them, and re-layouts  0.63 us (2%)
    pallas_call x1, Pallas kernels, per_device(): pl.pallas_call(main_kernel, out_shape=(jax.ShapeDtypeStruct(message, F32)...  31.3 us
    pallas_call x1, Pallas kernels, per_device(): pl.pallas_call(final_kernel, out_shape=(block, block, block, block, jax.S...  1.22 us

profile of v1, /device:TPU:1, one launch (start us, length us, event | category | flops | bytes accessed | tf_op | source)
XLA Modules:
  0.0 33.9 jit_solution(1464938491757203354)
XLA Ops:
  0.6 0.0 copy-start
  0.6 0.0 copy-start.1
  0.7 0.0 copy-start.2
  0.7 0.0 copy-start.3
  0.7 31.3 %spectral_exchange.1 = (f32[512,128]{1,0:T(8,128)S(1)}, f32[512,128]{1,0:T(8,128)S(1)}, f32[64,256]{1,0:T(8,128)S(1)}, f32[64,256]{1,0:T(8,128)S(1)}) custom-call(f32[2,256,128]{2,1,0:T(8,128)} %query.1, f32[2,256,128]{2,1,0:T(8,128)} %key.1, f32[2,256,128]{2,1,0:T(8,128)} %value.1, f32[2,256,128]{2,1,0:T(8,128)} %cotangent.1, f32[2,16384]{1,0:T(2,128)} %filters_hbm.1, ...), custom_call_target="tpu_custom_call" | custom-call | tf_op jit(solution)/shard_map/spectral_exchange/pallas_call | solution.py:341
  32.0 0.0 copy-start.4
  32.0 0.0 copy-done
  32.0 0.0 copy-done.1
  32.0 0.0 copy-done.2
  32.0 0.0 copy-done.3
  32.0 0.6 %copy-done.4 = f32[128]{0:T(128)S(1)} copy-done((f32[128]{0:T(128)S(1)}, f32[128]{0:T(128)}, u32[]{:S(2)}) %copy-start.4) | copy-done | bytes 536
  32.6 1.2 %gates.1 = (f32[2,256,128]{2,1,0:T(8,128)}, f32[2,256,128]{2,1,0:T(8,128)}, f32[2,256,128]{2,1,0:T(8,128)}, f32[2,256,128]{2,1,0:T(8,128)}, f32[2,8192]{1,0:T(2,128)}) custom-call(f32[512,128]{1,0:T(8,128)S(1)} %get-tuple-element.9.conv, f32[512,128]{1,0:T(8,128)S(1)} %get-tuple-element.10.back, f32[64,256]{1,0:T(8,128)S(1)} %get-tuple-element.11.lag_own, ...), custom_call_target="tpu_custom_call" | custom-call | tf_op jit(solution)/shard_map/gates/pallas_call | solution.py:372
Async XLA Ops:
  0.6 31.4 %copy-start = (f32[2,256,128]{2,1,0:T(8,128)S(1)}, f32[2,256,128]{2,1,0:T(8,128)}, u32[]{:S(2)}) copy-start(f32[2,256,128]{2,1,0:T(8,128)} %query.1) | copy-start | bytes 786436
  0.6 31.4 %copy-start.1 = (f32[2,256,128]{2,1,0:T(8,128)S(1)}, f32[2,256,128]{2,1,0:T(8,128)}, u32[]{:S(2)}) copy-start(f32[2,256,128]{2,1,0:T(8,128)} %key.1) | copy-start | bytes 786436
  0.7 31.4 %copy-start.2 = (f32[2,256,128]{2,1,0:T(8,128)S(1)}, f32[2,256,128]{2,1,0:T(8,128)}, u32[]{:S(2)}) copy-start(f32[2,256,128]{2,1,0:T(8,128)} %value.1) | copy-start | bytes 786436
  0.7 31.4 %copy-start.3 = (f32[2,256,128]{2,1,0:T(8,128)S(1)}, f32[2,256,128]{2,1,0:T(8,128)}, u32[]{:S(2)}) copy-start(f32[2,256,128]{2,1,0:T(8,128)} %cotangent.1) | copy-start | bytes 786436
  32.0 0.7 %copy-start.4 = (f32[128]{0:T(128)S(1)}, f32[128]{0:T(128)}, u32[]{:S(2)}) copy-start(f32[128]{0:T(128)} %param.17) | copy-start | bytes 1540

commit v2 on v0

--- a/solution.py
+++ b/solution.py
@@ -17,6 +17,21 @@
 K1 = 128
 K2 = 256
 FULL = K1 * K2
+
+
+AWAY = (0, 1, 2, 1)
+
+SHIFTS = sorted(
+    (
+        (y, z, x, core)
+        for y in range(4)
+        for z in range(2)
+        for x in range(4)
+        for core in range(2)
+        if (y, z, x, core) != (0, 0, 0, 0)
+    ),
+    key=lambda d: -(AWAY[d[0]] + 2 * d[1] + AWAY[d[2]]),
+)
 
 
 def split_np(table):
@@ -142,17 +157,17 @@
 
 
 def main_kernel(
-    query_hbm, key_hbm, value_hbm, cotangent_hbm, filters_hbm, *rest
+    query_hbm, key_hbm, value_hbm, cotangent_hbm, filters_hbm, skip_hbm, *rest
 ):
     table_hbm, rest = rest[:7], rest[7:]
-    conv_out, back_out, lag_own_out, lag_other_out = rest[:4]
-    rest = rest[4:]
-    query, key, value, cotangent, filters = rest[:5]
-    tables, rest = rest[5:12], rest[12:]
+    output, query_grad, key_grad, value_grad, filter_grad = rest[:5]
+    rest = rest[5:]
+    query, key, value, cotangent, filters, skip = rest[:6]
+    tables, rest = rest[6:13], rest[13:]
     (
-        mixed_send, up_send, mixed_got, up_got, conv_send, back_send,
+        mixed_send, up_send, mixed_got, up_got, conv_send, back_send, conv_got, back_got,
         filter_rows, filter_spec, mixed_spec, up_spec, pair, wide, lag, lag_got,
-        load_sem, send_sem, recv_sem, lag_sem, own_sem,
+        load_sem, send_sem, recv_sem, lag_sem,
     ) = rest
     b = lax.axis_index("batch")
     s = lax.axis_index("seq")
@@ -161,25 +176,26 @@
         pltpu.make_async_copy(src, dst, load_sem.at[i])
         for i, (src, dst) in enumerate(
             zip(
-                (key_hbm, value_hbm, query_hbm, cotangent_hbm, filters_hbm) + tuple(table_hbm),
-                (key, value, query, cotangent, filters) + tuple(tables),
+                (key_hbm, value_hbm, query_hbm, cotangent_hbm, filters_hbm, skip_hbm)
+                + tuple(table_hbm),
+                (key, value, query, cotangent, filters, skip) + tuple(tables),
             )
         )
     ]
     for load in loads:
         load.start()
 
-    def peer(i):
-        turn = lax.rem(i - 1 + s * 17, PEERS - 1) + 1
-        return lax.rem(s + turn * 23, PEERS)
+    places = (
+        [lax.rem(s // 16 + i, 4) * 16 for i in range(4)],
+        [lax.rem(s // 8 + i, 2) * 8 for i in range(2)],
+        [lax.rem(s // 2 + i, 4) * 2 for i in range(4)],
+        [lax.rem(s + i, 2) for i in range(2)],
+    )
+    peers = [sum(place[i] for place, i in zip(places, shift)) for shift in SHIFTS]
 
     barrier = pltpu.get_barrier_semaphore()
-
-    def greet(i, carry):
-        pl.semaphore_signal(barrier, inc=1, device_id=(b, peer(i)), device_id_type=MESH)
-        return carry
-
-    lax.fori_loop(1, PEERS, greet, 0)
+    for d in peers:
+        pl.semaphore_signal(barrier, inc=1, device_id=(b, d), device_id_type=MESH)
     pl.semaphore_signal(barrier, inc=1, device_id=(1 - b, s), device_id_type=MESH)
 
     for first, second, left, right, target in (
@@ -200,8 +216,7 @@
         return pl.ds(pl.multiple_of(i * ROWS, ROWS), ROWS)
 
     def send(source, target, k):
-        def one(i, carry):
-            d = peer(i)
+        for d in peers:
             pltpu.make_async_remote_copy(
                 src_ref=source.at[block(d)],
                 dst_ref=target.at[block(s)],
@@ -210,9 +225,7 @@
                 device_id=(b, d),
                 device_id_type=MESH,
             ).start()
-            return carry
-
-        lax.fori_loop(1, PEERS, one, 0)
+        target[block(s), :] = source[block(s), :]
 
     def settled(source, target, k):
         rows = pl.ds(0, (PEERS - 1) * ROWS)
@@ -227,8 +240,6 @@
 
     send(mixed_send, mixed_got, 0)
     send(up_send, up_got, 1)
-    mixed_got[block(s), :] = mixed_send[block(s), :]
-    up_got[block(s), :] = up_send[block(s), :]
 
     for load in loads[4:]:
         load.wait()
@@ -250,16 +261,12 @@
     settled(mixed_send, mixed_got, 0).wait_recv()
     forward(mixed_got, mixed_spec, pair, tables)
     spread(inverse(mixed_spec, filter_spec, False, pair, wide, tables, False), conv_send)
-    send(conv_send, conv_out, 2)
-    own_conv = pltpu.make_async_copy(conv_send.at[block(s)], conv_out.at[block(s)], own_sem.at[0])
-    own_conv.start()
+    send(conv_send, conv_got, 2)
 
     settled(up_send, up_got, 1).wait_recv()
     forward(up_got, up_spec, pair, tables)
     spread(inverse(filter_spec, up_spec, True, pair, wide, tables, False), back_send)
-    send(back_send, back_out, 3)
-    own_back = pltpu.make_async_copy(back_send.at[block(s)], back_out.at[block(s)], own_sem.at[1])
-    own_back.start()
+    send(back_send, back_got, 3)
 
     results = inverse(mixed_spec, up_spec, True, pair, wide, tables, True)
     for half in range(2):
@@ -274,91 +281,90 @@
         device_id_type=MESH,
     )
     lag_copy.start()
-    own_lag = pltpu.make_async_copy(lag.at[b], lag_own_out, own_sem.at[2])
-    own_lag.start()
+
+    gain = skip[...]
+    parts = [(bb, slice(h * 128, (h + 1) * 128), pl.ds(bb * 2 + h, 128, stride=4)) for bb in range(2) for h in range(2)]
+    settled(conv_send, conv_got, 2).wait_recv()
+    for bb, tokens, rows in parts:
+        hidden = conv_got[rows, :].T + gain * (key[bb, tokens, :] * value[bb, tokens, :])
+        output[bb, tokens, :] = query[bb, tokens, :] * hidden
+        query_grad[bb, tokens, :] = cotangent[bb, tokens, :] * hidden
+
     lag_copy.wait_recv()
-    other_lag = pltpu.make_async_copy(lag_got, lag_other_out, own_sem.at[3])
-    other_lag.start()
-
+    total = (lag[b] + lag_got[...]) * (1.0 / 128.0)
+    for c in range(2):
+        for n in range(32):
+            filter_grad[c : c + 1, n * K2 : (n + 1) * K2] = total[c * 32 + n : c * 32 + n + 1, :]
     settled(mixed_send, mixed_got, 0).wait_send()
     settled(up_send, up_got, 1).wait_send()
-    settled(conv_send, conv_out, 2).wait()
-    settled(back_send, back_out, 3).wait()
+    settled(conv_send, conv_got, 2).wait_send()
     lag_copy.wait_send()
-    own_conv.wait()
-    own_back.wait()
-    own_lag.wait()
-    other_lag.wait()
-
-
-def final_kernel(
-    conv, back, lag_own, lag_other, query, key, value, cotangent, skip,
-    output, query_grad, key_grad, value_grad, filter_grad,
-):
-    gain = skip[...]
-    for bb in range(2):
+
+    settled(back_send, back_got, 3).wait_recv()
+    for bb, tokens, rows in parts:
+        mixed_grad = back_got[rows, :].T + gain * (cotangent[bb, tokens, :] * query[bb, tokens, :])
+        key_grad[bb, tokens, :] = mixed_grad * value[bb, tokens, :]
+        value_grad[bb, tokens, :] = mixed_grad * key[bb, tokens, :]
+    settled(back_send, back_got, 3).wait_send()
+
+
+def store_kernel(*refs):
+    sources, targets, sem = refs[:5], refs[5:10], refs[10]
+    copies = []
+    for i in range(5):
         for half in range(2):
-            tokens = slice(half * 128, (half + 1) * 128)
-            q, k = query[bb, tokens, :], key[bb, tokens, :]
-            v, g = value[bb, tokens, :], cotangent[bb, tokens, :]
-            rows = pl.ds(bb * 2 + half, 128, stride=4)
-            hidden = conv[rows, :].T + gain * (k * v)
-            output[bb, tokens, :] = q * hidden
-            query_grad[bb, tokens, :] = g * hidden
-            mixed_grad = back[rows, :].T + gain * (g * q)
-            key_grad[bb, tokens, :] = mixed_grad * v
-            value_grad[bb, tokens, :] = mixed_grad * k
-    total = (lag_own[...] + lag_other[...]) * (1.0 / 128.0)
-    for c in range(2):
-        for n in range(32):
-            filter_grad[c : c + 1, n * K2 : (n + 1) * K2] = total[c * 32 + n : c * 32 + n + 1, :]
+            part = (half,) if i < 4 else (slice(None), pl.ds(half * 16 * K2, 16 * K2))
+            copies.append(
+                pltpu.make_async_copy(sources[i].at[part], targets[i].at[part], sem.at[i, half])
+            )
+    for copy in copies:
+        copy.start()
+    for copy in copies:
+        copy.wait()
 
 
 def per_device(query, key, value, filters, skip, cotangent):
     tables = [jnp.asarray(t) for t in make_tables()]
     message = (PEERS * ROWS, 128)
-    any_space = pl.BlockSpec(memory_space=pl.ANY)
-    in_vmem = pl.BlockSpec(memory_space=pltpu.VMEM)
+    in_hbm = pl.BlockSpec(memory_space=pltpu.HBM)
     vmem = pltpu.VMEM
     tokens = query.shape
-    conv, back, lag_own, lag_other = pl.pallas_call(
+    operands = (query, key, value, cotangent, filters, skip.reshape(1, -1), *tables)
+    block = jax.ShapeDtypeStruct(tokens, F32)
+    shapes = (block, block, block, block, jax.ShapeDtypeStruct((2, 32 * K2), F32))
+    results = pl.pallas_call(
         main_kernel,
-        out_shape=(
-            jax.ShapeDtypeStruct(message, F32),
-            jax.ShapeDtypeStruct(message, F32),
-            jax.ShapeDtypeStruct((64, K2), F32),
-            jax.ShapeDtypeStruct((64, K2), F32),
-        ),
-        in_specs=[any_space] * 12,
-        out_specs=(any_space,) * 4,
+        out_shape=shapes,
+        in_specs=[in_hbm] * len(operands),
+        out_specs=(pl.BlockSpec(memory_space=pltpu.VMEM),) * 5,
         scratch_shapes=[vmem(tokens, F32)] * 4
-        + [vmem(filters.shape, F32)]
+        + [vmem(filters.shape, F32), vmem((1, tokens[2]), F32)]
         + [vmem(t.shape, t.dtype) for t in tables]
-        + [vmem(message, F32)] * 6
+        + [vmem(message, F32)] * 8
         + [vmem((2 * PEERS, K2), F32)]
         + [vmem((2 * K1, 2 * K2), F32)] * 3
         + [vmem((4 * K1, 2 * K2), BF16), vmem((2 * K1, 2 * K2), F32)]
         + [vmem((2, 64, K2), F32), vmem((64, K2), F32)]
         + [
-            pltpu.SemaphoreType.DMA((12,)),
+            pltpu.SemaphoreType.DMA((len(operands),)),
             pltpu.SemaphoreType.DMA((4,)),
             pltpu.SemaphoreType.DMA((4,)),
             pltpu.SemaphoreType.DMA((2,)),
-            pltpu.SemaphoreType.DMA((4,)),
         ],
         compiler_params=pltpu.CompilerParams(
             collective_id=0, has_side_effects=True, vmem_limit_bytes=40 * 1024 * 1024
         ),
         name="spectral_exchange",
-    )(query, key, value, cotangent, filters, *tables)
-    block = jax.ShapeDtypeStruct(tokens, F32)
+    )(*[pltpu.with_memory_space_constraint(x, pltpu.HBM) for x in operands])
     return pl.pallas_call(
-        final_kernel,
-        out_shape=(block, block, block, block, jax.ShapeDtypeStruct((2, 32 * K2), F32)),
-        in_specs=[in_vmem] * 9,
-        out_specs=(in_vmem,) * 5,
-        name="gates",
-    )(conv, back, lag_own, lag_other, query, key, value, cotangent, skip.reshape(1, -1))
+        store_kernel,
+        out_shape=shapes,
+        in_specs=[pl.BlockSpec(memory_space=pltpu.VMEM)] * 5,
+        out_specs=(in_hbm,) * 5,
+        scratch_shapes=[pltpu.SemaphoreType.DMA((5, 2))],
+        compiler_params=pltpu.CompilerParams(vmem_limit_bytes=16 * 1024 * 1024),
+        name="store",
+    )(*results)
 
 
 def solution(mesh):

time: 49.8 us -> 30 us (0.60)
  local copies, waits for them, and re-layouts: 13.9 us -> 0 us
  Pallas kernels: 34.7 us -> 29.2 us
    unnamed x32 -> x0, local copies, waits for them, and re-layouts: 13.9 us -> none
    pallas_call x2, Pallas kernels: 34.7 us -> 29.2 us  [the longest x1 28.1 us: per_device(): pl.pallas_call(main_kernel, out_shape=shapes, in_specs=[in_hbm] * len(ope...]
where the time goes in v2:
time: 30 us; the launch traced here: 29.8 us
  Pallas kernels  29.2 us (97%)
  between operations  0.64 us (2%)
    pallas_call x1, Pallas kernels, per_device(): pl.pallas_call(main_kernel, out_shape=shapes, in_specs=[in_hbm] * len(ope...  28.1 us
    pallas_call x1, Pallas kernels, per_device(): pl.pallas_call(store_kernel, out_shape=shapes, in_specs=[pl.BlockSpec(mem...  1.06 us

profile of v2, /device:TPU:1, one launch (start us, length us, event | category | flops | bytes accessed | tf_op | source)
XLA Modules:
  0.0 29.8 jit_solution(2862369977673194744)
XLA Ops:
  0.6 28.1 %spectral_exchange.1 = (f32[2,256,128]{2,1,0:T(8,128)S(1)}, f32[2,256,128]{2,1,0:T(8,128)S(1)}, f32[2,256,128]{2,1,0:T(8,128)S(1)}, f32[2,256,128]{2,1,0:T(8,128)S(1)}, f32[2,8192]{1,0:T(2,128)S(1)}) custom-call(f32[2,256,128]{2,1,0:T(8,128)} %query_hbm.1, f32[2,256,128]{2,1,0:T(8,128)} %key_hbm.1, f32[2,256,128]{2,1,0:T(8,128)} %value_hbm.1, ...), custom_call_target="tpu_custom_call" | custom-call | tf_op jit(solution)/shard_map/spectral_exchange/pallas_call | solution.py:335
  28.8 1.1 %store.1 = (f32[2,256,128]{2,1,0:T(8,128)}, f32[2,256,128]{2,1,0:T(8,128)}, f32[2,256,128]{2,1,0:T(8,128)}, f32[2,256,128]{2,1,0:T(8,128)}, f32[2,8192]{1,0:T(2,128)}) custom-call(f32[2,256,128]{2,1,0:T(8,128)S(1)} %get-tuple-element.10.refs_0_, f32[2,256,128]{2,1,0:T(8,128)S(1)} %get-tuple-element.11.refs_1_, f32[2,256,128]{2,1,0:T(8,128)S(1)} %get-tuple-element.12.refs_2_, ...), custom_call_target="tpu_custom_call" | custom-call | tf_op jit(solution)/shard_map/store/pallas_call | solution.py:359

commit v3 on v2

v3 whole, which is shorter than its diff:
```python
import functools

import jax
import jax.numpy as jnp
import numpy as np
from jax import lax
from jax.experimental import pallas as pl
from jax.experimental.pallas import tpu as pltpu
from jax.sharding import PartitionSpec as P

MESH = pl.DeviceIdType.MESH
F32 = jnp.float32
BF16 = jnp.bfloat16

PEERS = 64
ROWS = 8
K1 = 128
K2 = 256
HALF = K2 // 2
FULL = K1 * K2
PART = 4


AWAY = (0, 1, 2, 1)

SHIFTS = sorted(
    ((y, z, x) for y in range(4) for z in range(2) for x in range(4) if (y, z, x) != (0, 0, 0)),
    key=lambda d: -(AWAY[d[0]] + 2 * d[1] + AWAY[d[2]]),
)


MIXED_CHUNKS = ((0,), (1,))
UP_CHUNKS = ((0, 1),)


def split_np(table):
    hi = table.astype(BF16)
    lo = (table - hi.astype(np.float64)).astype(BF16)
    return hi, lo


def rotation(angle):
    c, s = np.cos(angle), np.sin(angle)
    return np.block([[c, -s], [s, c]])


def make_tables():
    k1 = np.arange(K1)
    n1 = np.arange(PEERS)
    n2 = np.arange(K2)
    half = np.arange(HALF)
    left = rotation(2.0 * np.pi * (np.outer(n1, k1) % K1) / K1).T
    left_hi, left_lo = split_np(left)
    left_all = np.concatenate([left_hi, left_hi, left_lo], axis=1)
    left_filter = np.concatenate(
        [left_hi[:, :PEERS], left_hi[:, :PEERS], left_lo[:, :PEERS]], axis=1
    )
    inv_hi, inv_lo = split_np(left.T / FULL)
    inv = np.concatenate([inv_hi, inv_hi, inv_lo], axis=1)
    even = 2.0 * np.pi * (np.outer(half, 2 * half) % K2) / K2
    odd = 2.0 * np.pi * (np.outer(half, 2 * half + 1) % K2) / K2
    right = []
    for angle in (even, odd, odd.T):
        hi, lo = split_np(rotation(angle))
        right.append(np.concatenate([hi, hi, lo], axis=0))
    angle = 2.0 * np.pi * (np.outer(k1, n2) % FULL) / FULL
    twist = np.concatenate([np.cos(angle), np.sin(angle)], axis=0).astype(np.float32)
    return (left_all, left_filter, inv, twist, np.stack(right))


def halves(x):
    hi = x.astype(BF16)
    lo = (x - hi.astype(F32)).astype(BF16)
    return hi, lo


def dot(a, b):
    return jnp.dot(a, b, preferred_element_type=F32)


def turn_forward(section, twist):
    re, im = section[:K1], section[K1:]
    tc, ts = twist[:K1], twist[K1:]
    return re * tc + im * ts, im * tc - re * ts


def turn_inverse(re, im, twist):
    tc, ts = twist[:K1], twist[K1:]
    return re * tc - im * ts, im * tc + re * ts


def second_stage(re, im, right):
    hi, lo = halves(jnp.concatenate([re, im], axis=1))
    return dot(jnp.concatenate([hi, lo, hi], axis=1), right)


def split_stage(turned, right):
    res = jnp.concatenate([t[0] for t in turned], axis=0)
    ims = jnp.concatenate([t[1] for t in turned], axis=0)
    even = second_stage(res[:, :HALF] + res[:, HALF:], ims[:, :HALF] + ims[:, HALF:], right[0])
    odd = second_stage(res[:, :HALF] - res[:, HALF:], ims[:, :HALF] - ims[:, HALF:], right[1])
    return even, odd


def gather_rows(block_ref, row):
    return block_ref[pl.ds(row, PEERS, stride=ROWS), :]


def store_spectrum(spec_ref, channels, turned, right):
    rows = slice(channels[0] * K1, (channels[-1] + 1) * K1)
    spec_ref[rows, :K2], spec_ref[rows, K2:] = split_stage(turned, right)


def forward(block_ref, spec_ref, channels, tables):
    left_all, _, _, twist, right = tables
    turned = []
    for c in channels:
        values = [
            jnp.concatenate(
                [gather_rows(block_ref, c * 4 + b * 2), gather_rows(block_ref, c * 4 + b * 2 + 1)],
                axis=1,
            )
            for b in range(2)
        ]
        hi, lo = halves(jnp.concatenate(values, axis=0))
        section = dot(left_all[...], jnp.concatenate([hi, lo, hi], axis=0))
        turned.append(turn_forward(section, twist))
    store_spectrum(spec_ref, channels, turned, right)


def forward_filters(rows_ref, spec_ref, tables):
    _, left_filter, _, twist, right = tables
    turned = []
    for c in range(2):
        hi, lo = halves(rows_ref[c * PEERS : (c + 1) * PEERS, :])
        section = dot(left_filter[...], jnp.concatenate([hi, lo, hi], axis=0))
        turned.append(turn_forward(section, twist))
    store_spectrum(spec_ref, (0, 1), turned, right)


def multiply(left_ref, right_ref, c, parity, conjugate_left):
    rows = slice(c * K1, (c + 1) * K1)
    re = slice(parity * K2, parity * K2 + HALF)
    im = slice(parity * K2 + HALF, (parity + 1) * K2)
    lr, li = left_ref[rows, re], left_ref[rows, im]
    rr, ri = right_ref[rows, re], right_ref[rows, im]
    if conjugate_left:
        return lr * rr + li * ri, lr * ri - li * rr
    return lr * rr - li * ri, lr * ri + li * rr


def inverse(left_ref, right_ref, channels, conjugate_left, tables, real_only):
    _, _, inv, twist, right = tables
    parts = []
    for parity, k in ((0, 0), (1, 2)):
        products = [multiply(left_ref, right_ref, c, parity, conjugate_left) for c in channels]
        res = jnp.concatenate([p[0] for p in products], axis=0)
        ims = jnp.concatenate([p[1] for p in products], axis=0)
        parts.append(second_stage(ims, res, right[k]))
    even, odd = parts
    first, second = even + odd, even - odd
    results = []
    for i in range(len(channels)):
        r = slice(i * K1, (i + 1) * K1)
        im = jnp.concatenate([first[r, :HALF], second[r, :HALF]], axis=1)
        re = jnp.concatenate([first[r, HALF:], second[r, HALF:]], axis=1)
        re, im = turn_inverse(re, im, twist)
        hi, lo = halves(jnp.concatenate([re, im], axis=0))
        rows = PEERS if real_only else 2 * PEERS
        results.append(dot(inv[:rows, :], jnp.concatenate([hi, lo, hi], axis=0)))
    return results


def main_kernel(
    query_hbm, key_hbm, value_hbm, cotangent_hbm, filters_hbm, skip_hbm, *rest
):
    table_hbm, rest = rest[:5], rest[5:]
    output, query_grad, key_grad, value_grad, filter_grad = rest[:5]
    rest = rest[5:]
    query, key, value, cotangent, filters, skip = rest[:6]
    tables, rest = rest[6:11], rest[11:]
    (
        mixed_send, up_send, mixed_got, up_got, conv_send, back_send, conv_got, back_got,
        filter_rows, filter_spec, mixed_spec, up_spec, lag, lag_got,
        load_sem, send_sem, recv_sem, lag_sem,
    ) = rest
    b = lax.axis_index("batch")
    s = lax.axis_index("seq")

    loads = [
        pltpu.make_async_copy(src, dst, load_sem.at[i])
        for i, (src, dst) in enumerate(
            zip(
                (key_hbm, value_hbm, query_hbm, cotangent_hbm, filters_hbm, skip_hbm)
                + tuple(table_hbm),
                (key, value, query, cotangent, filters, skip) + tuple(tables),
            )
        )
    ]
    for load in loads:
        load.start()

    places = (
        [lax.rem(s // 16 + i, 4) * 16 for i in range(4)],
        [lax.rem(s // 8 + i, 2) * 8 for i in range(2)],
        [lax.rem(s // 2 + i, 4) * 2 for i in range(4)],
    )
    core = lax.rem(s, 2)
    own = s - core
    chips = [sum(place[i] for place, i in zip(places, shift)) for shift in SHIFTS]
    peers = [chip + i for chip in chips for i in range(2)] + [own + 1 - core]
    early = [jnp.where(own == 0, chips[0], 0)] + [jnp.where(chip == 0, chips[0], chip) for chip in chips[1:]]
    early_peers = [chip + i for chip in early for i in range(2)] + [own + 1 - core]

    barrier = pltpu.get_barrier_semaphore()
    for d in peers:
        pl.semaphore_signal(barrier, inc=1, device_id=(b, d), device_id_type=MESH)
    pl.semaphore_signal(barrier, inc=1, device_id=(1 - b, s), device_id_type=MESH)

    for first, second, left, right, target in (
        (0, 1, key, value, mixed_send),
        (2, 3, query, cotangent, up_send),
    ):
        loads[first].wait()
        loads[second].wait()
        for bb in range(2):
            for half in range(2):
                tokens = slice(half * 128, (half + 1) * 128)
                product = left[bb, tokens, :] * right[bb, tokens, :]
                target[pl.ds(bb * 2 + half, 128, stride=4), :] = product.T

    pl.semaphore_wait(barrier, PEERS)

    def block(i, channels):
        rows = len(channels) * PART
        return pl.ds(pl.multiple_of(i * ROWS + channels[0] * PART, rows), rows)

    def send(source, target, k, channels, partners):
        for d in partners:
            pltpu.make_async_remote_copy(
                src_ref=source.at[block(d, channels)],
                dst_ref=target.at[block(s, channels)],
                send_sem=send_sem.at[k, channels[0]],
                recv_sem=recv_sem.at[k, channels[0]],
                device_id=(b, d),
                device_id_type=MESH,
            ).start()
        target[block(s, channels), :] = source[block(s, channels), :]

    def settled(source, target, k, channels):
        rows = pl.ds(0, (PEERS - 1) * PART * len(channels))
        return pltpu.make_async_remote_copy(
            src_ref=source.at[rows],
            dst_ref=target.at[rows],
            send_sem=send_sem.at[k, channels[0]],
            recv_sem=recv_sem.at[k, channels[0]],
            device_id=(1 - b, s),
            device_id_type=MESH,
        )

    for channels in MIXED_CHUNKS:
        send(mixed_send, mixed_got, 0, channels, peers)
    for channels in UP_CHUNKS:
        send(up_send, up_got, 1, channels, peers)

    for load in loads[4:]:
        load.wait()
    for c in range(2):
        for n1 in range(PEERS):
            filter_rows[c * PEERS + n1 : c * PEERS + n1 + 1, :] = filters[
                c : c + 1, n1 * K2 : (n1 + 1) * K2
            ]
    forward_filters(filter_rows, filter_spec, tables)

    def spread(results, target, channels):
        for result, c in zip(results, channels):
            for bb in range(2):
                for half in range(2):
                    target[pl.ds(c * 4 + bb * 2 + half, PEERS, stride=ROWS), :] = result[
                        bb * PEERS : (bb + 1) * PEERS, half * 128 : (half + 1) * 128
                    ]

    for channels in MIXED_CHUNKS:
        settled(mixed_send, mixed_got, 0, channels).wait_recv()
        forward(mixed_got, mixed_spec, channels, tables)
        spread(inverse(mixed_spec, filter_spec, channels, False, tables, False), conv_send, channels)
        send(conv_send, conv_got, 2, channels, early_peers)
    for channels in UP_CHUNKS:
        settled(up_send, up_got, 1, channels).wait_recv()
        forward(up_got, up_spec, channels, tables)
        spread(inverse(filter_spec, up_spec, channels, True, tables, False), back_send, channels)
        send(back_send, back_got, 3, channels, early_peers)

    result = inverse(mixed_spec, up_spec, (0, 1), True, tables, True)
    for half in range(2):
        for c in range(2):
            lag[half, c * 32 : (c + 1) * 32, :] = result[c][half * 32 : (half + 1) * 32, :]
    lag_copy = pltpu.make_async_remote_copy(
        src_ref=lag.at[1 - b],
        dst_ref=lag_got,
        send_sem=lag_sem.at[0],
        recv_sem=lag_sem.at[1],
        device_id=(1 - b, s),
        device_id_type=MESH,
    )
    lag_copy.start()

    gain = skip[...]
    parts = [(bb, slice(h * 128, (h + 1) * 128), pl.ds(bb * 2 + h, 128, stride=4)) for bb in range(2) for h in range(2)]
    for channels in MIXED_CHUNKS:
        settled(conv_send, conv_got, 2, channels).wait_recv()
    for bb, tokens, rows in parts:
        hidden = conv_got[rows, :].T + gain * (key[bb, tokens, :] * value[bb, tokens, :])
        output[bb, tokens, :] = query[bb, tokens, :] * hidden
        query_grad[bb, tokens, :] = cotangent[bb, tokens, :] * hidden

    lag_copy.wait_recv()
    total = (lag[b] + lag_got[...]) * (1.0 / 128.0)
    for c in range(2):
        for n in range(32):
            filter_grad[c : c + 1, n * K2 : (n + 1) * K2] = total[c * 32 + n : c * 32 + n + 1, :]
    for channels in MIXED_CHUNKS:
        settled(mixed_send, mixed_got, 0, channels).wait_send()
        settled(conv_send, conv_got, 2, channels).wait_send()
    for channels in UP_CHUNKS:
        settled(up_send, up_got, 1, channels).wait_send()
    lag_copy.wait_send()

    for channels in UP_CHUNKS:
        settled(back_send, back_got, 3, channels).wait_recv()
    for bb, tokens, rows in parts:
        mixed_grad = back_got[rows, :].T + gain * (cotangent[bb, tokens, :] * query[bb, tokens, :])
        key_grad[bb, tokens, :] = mixed_grad * value[bb, tokens, :]
        value_grad[bb, tokens, :] = mixed_grad * key[bb, tokens, :]
    for channels in UP_CHUNKS:
        settled(back_send, back_got, 3, channels).wait_send()


def store_kernel(*refs):
    sources, targets, sem = refs[:5], refs[5:10], refs[10]
    copies = []
    for i in range(5):
        for half in range(2):
            part = (half,) if i < 4 else (slice(None), pl.ds(half * 16 * K2, 16 * K2))
            copies.append(
                pltpu.make_async_copy(sources[i].at[part], targets[i].at[part], sem.at[i, half])
            )
    for copy in copies:
        copy.start()
    for copy in copies:
        copy.wait()


def per_device(query, key, value, filters, skip, cotangent):
    tables = [jnp.asarray(t) for t in make_tables()]
    message = (PEERS * ROWS, 128)
    in_hbm = pl.BlockSpec(memory_space=pltpu.HBM)
    vmem = pltpu.VMEM
    tokens = query.shape
    operands = (query, key, value, cotangent, filters, skip.reshape(1, -1), *tables)
    block = jax.ShapeDtypeStruct(tokens, F32)
    shapes = (block, block, block, block, jax.ShapeDtypeStruct((2, 32 * K2), F32))
    results = pl.pallas_call(
        main_kernel,
        out_shape=shapes,
        in_specs=[in_hbm] * len(operands),
        out_specs=(pl.BlockSpec(memory_space=pltpu.VMEM),) * 5,
        scratch_shapes=[vmem(tokens, F32)] * 4
        + [vmem(filters.shape, F32), vmem((1, tokens[2]), F32)]
        + [vmem(t.shape, t.dtype) for t in tables]
        + [vmem(message, F32)] * 8
        + [vmem((2 * PEERS, K2), F32)]
        + [vmem((2 * K1, 2 * K2), F32)] * 3
        + [vmem((2, 64, K2), F32), vmem((64, K2), F32)]
        + [
            pltpu.SemaphoreType.DMA((len(operands),)),
            pltpu.SemaphoreType.DMA((4, 2)),
            pltpu.SemaphoreType.DMA((4, 2)),
            pltpu.SemaphoreType.DMA((2,)),
        ],
        compiler_params=pltpu.CompilerParams(
            collective_id=0, has_side_effects=True, vmem_limit_bytes=40 * 1024 * 1024
        ),
        name="spectral_exchange",
    )(*[pltpu.with_memory_space_constraint(x, pltpu.HBM) for x in operands])
    return pl.pallas_call(
        store_kernel,
        out_shape=shapes,
        in_specs=[pl.BlockSpec(memory_space=pltpu.VMEM)] * 5,
        out_specs=(in_hbm,) * 5,
        scratch_shapes=[pltpu.SemaphoreType.DMA((5, 2))],
        compiler_params=pltpu.CompilerParams(vmem_limit_bytes=16 * 1024 * 1024),
        name="store",
    )(*results)


def solution(mesh):
    rows = P("batch", "seq", None)
    return jax.shard_map(
        per_device,
        mesh=mesh,
        in_specs=(rows, rows, rows, P("seq", None), P(), rows),
        out_specs=(rows, rows, rows, rows, P("seq", "batch")),
        check_vma=False,
    )
```

time: 30 us -> 29.2 us (0.973)
  Pallas kernels: 29.2 us -> 28.5 us
    pallas_call x1, Pallas kernels: 28.1 us -> 27.4 us  [per_device(): pl.pallas_call(main_kernel, out_shape=shapes, in_specs=[in_hbm] * len(ope...]
where the time goes in v3:
time: 29.2 us; the launch traced here: 29.1 us
  Pallas kernels  28.5 us (98%)
  between operations  0.64 us (2%)
    pallas_call x1, Pallas kernels, per_device(): pl.pallas_call(main_kernel, out_shape=shapes, in_specs=[in_hbm] * len(ope...  27.4 us
    pallas_call x1, Pallas kernels, per_device(): pl.pallas_call(store_kernel, out_shape=shapes, in_specs=[pl.BlockSpec(mem...  1.06 us

profile of v3, /device:TPU:1, one launch (start us, length us, event | category | flops | bytes accessed | tf_op | source)
XLA Modules:
  0.0 29.1 jit_solution(936828117130632236)
XLA Ops:
  0.6 27.4 %spectral_exchange.1 = (f32[2,256,128]{2,1,0:T(8,128)S(1)}, f32[2,256,128]{2,1,0:T(8,128)S(1)}, f32[2,256,128]{2,1,0:T(8,128)S(1)}, f32[2,256,128]{2,1,0:T(8,128)S(1)}, f32[2,8192]{1,0:T(2,128)S(1)}) custom-call(f32[2,256,128]{2,1,0:T(8,128)} %query_hbm.1, f32[2,256,128]{2,1,0:T(8,128)} %key_hbm.1, f32[2,256,128]{2,1,0:T(8,128)} %value_hbm.1, ...), custom_call_target="tpu_custom_call" | custom-call | tf_op jit(solution)/shard_map/spectral_exchange/pallas_call | solution.py:363
  28.1 1.1 %store.1 = (f32[2,256,128]{2,1,0:T(8,128)}, f32[2,256,128]{2,1,0:T(8,128)}, f32[2,256,128]{2,1,0:T(8,128)}, f32[2,256,128]{2,1,0:T(8,128)}, f32[2,8192]{1,0:T(2,128)}) custom-call(f32[2,256,128]{2,1,0:T(8,128)S(1)} %get-tuple-element.10.refs_0_, f32[2,256,128]{2,1,0:T(8,128)S(1)} %get-tuple-element.11.refs_1_, f32[2,256,128]{2,1,0:T(8,128)S(1)} %get-tuple-element.12.refs_2_, ...), custom_call_target="tpu_custom_call" | custom-call | tf_op jit(solution)/shard_map/store/pallas_call | solution.py:386

commit v4 on v3

--- a/solution.py
+++ b/solution.py
@@ -45,17 +45,18 @@
 
 
 def make_tables():
-    k1 = np.arange(K1)
+    pair = np.arange(PEERS)
     n1 = np.arange(PEERS)
     n2 = np.arange(K2)
     half = np.arange(HALF)
-    left = rotation(2.0 * np.pi * (np.outer(n1, k1) % K1) / K1).T
-    left_hi, left_lo = split_np(left)
-    left_all = np.concatenate([left_hi, left_hi, left_lo], axis=1)
-    left_filter = np.concatenate(
-        [left_hi[:, :PEERS], left_hi[:, :PEERS], left_lo[:, :PEERS]], axis=1
-    )
-    inv_hi, inv_lo = split_np(left.T / FULL)
+    angle = 2.0 * np.pi * (np.outer(pair, n1) % K1) / K1
+    cosine, sine = np.cos(angle), np.sin(angle)
+    alternate = np.where(n1 % 2 == 0, 1.0, -1.0)
+    sine[0] = alternate
+    left_hi, left_lo = split_np(np.concatenate([cosine, sine], axis=0))
+    left = np.concatenate([left_hi, left_hi, left_lo], axis=1)
+    sine[0] = -alternate
+    inv_hi, inv_lo = split_np(np.concatenate([cosine, -sine], axis=0).T / FULL)
     inv = np.concatenate([inv_hi, inv_hi, inv_lo], axis=1)
     even = 2.0 * np.pi * (np.outer(half, 2 * half) % K2) / K2
     odd = 2.0 * np.pi * (np.outer(half, 2 * half + 1) % K2) / K2
@@ -63,9 +64,10 @@
     for angle in (even, odd, odd.T):
         hi, lo = split_np(rotation(angle))
         right.append(np.concatenate([hi, hi, lo], axis=0))
-    angle = 2.0 * np.pi * (np.outer(k1, n2) % FULL) / FULL
+    bins = np.concatenate([pair, [PEERS], K1 - pair[1:]])
+    angle = 2.0 * np.pi * (np.outer(bins, n2) % FULL) / FULL
     twist = np.concatenate([np.cos(angle), np.sin(angle)], axis=0).astype(np.float32)
-    return (left_all, left_filter, inv, twist, np.stack(right))
+    return (left, inv, twist, np.stack(right))
 
 
 def halves(x):
@@ -78,8 +80,7 @@
     return jnp.dot(a, b, preferred_element_type=F32)
 
 
-def turn_forward(section, twist):
-    re, im = section[:K1], section[K1:]
+def turn_forward(re, im, twist):
     tc, ts = twist[:K1], twist[K1:]
     return re * tc + im * ts, im * tc - re * ts
 
@@ -111,8 +112,18 @@
     spec_ref[rows, :K2], spec_ref[rows, K2:] = split_stage(turned, right)
 
 
+def first_row():
+    return lax.broadcasted_iota(jnp.int32, (PEERS, K2), 0) == 0
+
+
+def first_stage(left, first, second):
+    hi, lo = halves(jnp.concatenate([first, second], axis=1))
+    both = dot(left[...], jnp.concatenate([hi, lo, hi], axis=0))
+    return both[:PEERS, :K2], both[PEERS:, :K2], both[:PEERS, K2:], both[PEERS:, K2:]
+
+
 def forward(block_ref, spec_ref, channels, tables):
-    left_all, _, _, twist, right = tables
+    left, _, twist, right = tables
     turned = []
     for c in channels:
         values = [
@@ -122,19 +133,23 @@
             )
             for b in range(2)
         ]
-        hi, lo = halves(jnp.concatenate(values, axis=0))
-        section = dot(left_all[...], jnp.concatenate([hi, lo, hi], axis=0))
-        turned.append(turn_forward(section, twist))
+        cos0, sin0, cos1, sin1 = first_stage(left, *values)
+        row = first_row()
+        re = [cos0 + jnp.where(row, 0.0, sin1), jnp.where(row, sin0, cos0 - sin1)]
+        im = [cos1 - jnp.where(row, 0.0, sin0), jnp.where(row, sin1, cos1 + sin0)]
+        turned.append(turn_forward(jnp.concatenate(re, axis=0), jnp.concatenate(im, axis=0), twist))
     store_spectrum(spec_ref, channels, turned, right)
 
 
 def forward_filters(rows_ref, spec_ref, tables):
-    _, left_filter, _, twist, right = tables
+    left, _, twist, right = tables
+    cos0, sin0, cos1, sin1 = first_stage(left, rows_ref[:PEERS, :], rows_ref[PEERS:, :])
     turned = []
-    for c in range(2):
-        hi, lo = halves(rows_ref[c * PEERS : (c + 1) * PEERS, :])
-        section = dot(left_filter[...], jnp.concatenate([hi, lo, hi], axis=0))
-        turned.append(turn_forward(section, twist))
+    for cosine, sine in ((cos0, sin0), (cos1, sin1)):
+        row = first_row()
+        im = jnp.where(row, 0.0, sine)
+        re = jnp.concatenate([cosine, jnp.where(row, sine, cosine)], axis=0)
+        turned.append(turn_forward(re, jnp.concatenate([-im, im], axis=0), twist))
     store_spectrum(spec_ref, (0, 1), turned, right)
 
 
@@ -150,7 +165,7 @@
 
 
 def inverse(left_ref, right_ref, channels, conjugate_left, tables, real_only):
-    _, _, inv, twist, right = tables
+    _, inv, twist, right = tables
     parts = []
     for parity, k in ((0, 0), (1, 2)):
         products = [multiply(left_ref, right_ref, c, parity, conjugate_left) for c in channels]
@@ -165,20 +180,37 @@
         im = jnp.concatenate([first[r, :HALF], second[r, :HALF]], axis=1)
         re = jnp.concatenate([first[r, HALF:], second[r, HALF:]], axis=1)
         re, im = turn_inverse(re, im, twist)
-        hi, lo = halves(jnp.concatenate([re, im], axis=0))
-        rows = PEERS if real_only else 2 * PEERS
-        results.append(dot(inv[:rows, :], jnp.concatenate([hi, lo, hi], axis=0)))
+        row = first_row()
+        re_up, re_down, im_up, im_down = re[:PEERS], re[PEERS:], im[:PEERS], im[PEERS:]
+        folded = jnp.concatenate(
+            [
+                jnp.where(row, re_up, re_up + re_down),
+                jnp.where(row, re_down, im_up - im_down),
+            ],
+            axis=0,
+        )
+        if not real_only:
+            other = jnp.concatenate(
+                [
+                    jnp.where(row, im_up, im_up + im_down),
+                    jnp.where(row, im_down, re_down - re_up),
+                ],
+                axis=0,
+            )
+            folded = jnp.concatenate([folded, other], axis=1)
+        hi, lo = halves(folded)
+        results.append(dot(inv[...], jnp.concatenate([hi, lo, hi], axis=0)))
     return results
 
 
 def main_kernel(
     query_hbm, key_hbm, value_hbm, cotangent_hbm, filters_hbm, skip_hbm, *rest
 ):
-    table_hbm, rest = rest[:5], rest[5:]
+    table_hbm, rest = rest[:4], rest[4:]
     output, query_grad, key_grad, value_grad, filter_grad = rest[:5]
     rest = rest[5:]
     query, key, value, cotangent, filters, skip = rest[:6]
-    tables, rest = rest[6:11], rest[11:]
+    tables, rest = rest[6:10], rest[10:]
     (
         mixed_send, up_send, mixed_got, up_got, conv_send, back_send, conv_got, back_got,
         filter_rows, filter_spec, mixed_spec, up_spec, lag, lag_got,
@@ -276,9 +308,8 @@
         for result, c in zip(results, channels):
             for bb in range(2):
                 for half in range(2):
-                    target[pl.ds(c * 4 + bb * 2 + half, PEERS, stride=ROWS), :] = result[
-                        bb * PEERS : (bb + 1) * PEERS, half * 128 : (half + 1) * 128
-                    ]
+                    lanes = slice(bb * K2 + half * 128, bb * K2 + (half + 1) * 128)
+                    target[pl.ds(c * 4 + bb * 2 + half, PEERS, stride=ROWS), :] = result[:, lanes]
 
     for channels in MIXED_CHUNKS:
         settled(mixed_send, mixed_got, 0, channels).wait_recv()

time: 29.2 us -> 29 us (level)
  Pallas kernels: 28.5 us -> 28.2 us
where the time goes in v4:
time: 29 us; the launch traced here: 28.9 us
  Pallas kernels  28.2 us (97%)
  between operations  0.64 us (2%)
    pallas_call x1, Pallas kernels, per_device(): pl.pallas_call(main_kernel, out_shape=shapes, in_specs=[in_hbm] * len(ope...  27.2 us
    pallas_call x1, Pallas kernels, per_device(): pl.pallas_call(store_kernel, out_shape=shapes, in_specs=[pl.BlockSpec(mem...  1.06 us

profile of v4, /device:TPU:1, one launch (start us, length us, event | category | flops | bytes accessed | tf_op | source)
XLA Modules:
  0.0 28.9 jit_solution(5215654496701045511)
XLA Ops:
  0.6 27.2 %spectral_exchange.1 = (f32[2,256,128]{2,1,0:T(8,128)S(1)}, f32[2,256,128]{2,1,0:T(8,128)S(1)}, f32[2,256,128]{2,1,0:T(8,128)S(1)}, f32[2,256,128]{2,1,0:T(8,128)S(1)}, f32[2,8192]{1,0:T(2,128)S(1)}) custom-call(f32[2,256,128]{2,1,0:T(8,128)} %query_hbm.1, f32[2,256,128]{2,1,0:T(8,128)} %key_hbm.1, f32[2,256,128]{2,1,0:T(8,128)} %value_hbm.1, ...), custom_call_target="tpu_custom_call" | custom-call | tf_op jit(solution)/shard_map/spectral_exchange/pallas_call | solution.py:394
  27.8 1.1 %store.1 = (f32[2,256,128]{2,1,0:T(8,128)}, f32[2,256,128]{2,1,0:T(8,128)}, f32[2,256,128]{2,1,0:T(8,128)}, f32[2,256,128]{2,1,0:T(8,128)}, f32[2,8192]{1,0:T(2,128)}) custom-call(f32[2,256,128]{2,1,0:T(8,128)S(1)} %get-tuple-element.10.refs_0_, f32[2,256,128]{2,1,0:T(8,128)S(1)} %get-tuple-element.11.refs_1_, f32[2,256,128]{2,1,0:T(8,128)S(1)} %get-tuple-element.12.refs_2_, ...), custom_call_target="tpu_custom_call" | custom-call | tf_op jit(solution)/shard_map/store/pallas_call | solution.py:417

commit v5 on v4

--- a/solution.py
+++ b/solution.py
@@ -166,14 +166,19 @@
 
 def inverse(left_ref, right_ref, channels, conjugate_left, tables, real_only):
     _, inv, twist, right = tables
-    parts = []
-    for parity, k in ((0, 0), (1, 2)):
+    stacks = []
+    for parity in range(2):
         products = [multiply(left_ref, right_ref, c, parity, conjugate_left) for c in channels]
         res = jnp.concatenate([p[0] for p in products], axis=0)
         ims = jnp.concatenate([p[1] for p in products], axis=0)
-        parts.append(second_stage(ims, res, right[k]))
-    even, odd = parts
-    first, second = even + odd, even - odd
+        stacks.append(halves(jnp.concatenate([ims, res], axis=1)))
+    outs = []
+    for i in range(len(channels)):
+        r = slice(i * K1, (i + 1) * K1)
+        e, o = [dot(jnp.concatenate([hi[r], lo[r], hi[r]], axis=1), right[k]) for (hi, lo), k in zip(stacks, (0, 2))]
+        outs.append((e + o, e - o))
+    first = jnp.concatenate([x[0] for x in outs], axis=0)
+    second = jnp.concatenate([x[1] for x in outs], axis=0)
     results = []
     for i in range(len(channels)):
         r = slice(i * K1, (i + 1) * K1)
@@ -315,7 +320,7 @@
         settled(mixed_send, mixed_got, 0, channels).wait_recv()
         forward(mixed_got, mixed_spec, channels, tables)
         spread(inverse(mixed_spec, filter_spec, channels, False, tables, False), conv_send, channels)
-        send(conv_send, conv_got, 2, channels, early_peers)
+        send(conv_send, conv_got, 2, channels, peers)
     for channels in UP_CHUNKS:
         settled(up_send, up_got, 1, channels).wait_recv()
         forward(up_got, up_spec, channels, tables)

time: 29 us -> 28.8 us (level)
  no operation moved by 1% of the time
where the time goes in v5:
time: 28.8 us; the launch traced here: 28.7 us
  Pallas kernels  28.1 us (98%)
  between operations  0.64 us (2%)
    pallas_call x1, Pallas kernels, per_device(): pl.pallas_call(main_kernel, out_shape=shapes, in_specs=[in_hbm] * len(ope...  27 us
    pallas_call x1, Pallas kernels, per_device(): pl.pallas_call(store_kernel, out_shape=shapes, in_specs=[pl.BlockSpec(mem...  1.06 us

profile of v5, /device:TPU:1, one launch (start us, length us, event | category | flops | bytes accessed | tf_op | source)
XLA Modules:
  0.0 28.7 jit_solution(12896278516905640198)
XLA Ops:
  0.6 27.0 %spectral_exchange.1 = (f32[2,256,128]{2,1,0:T(8,128)S(1)}, f32[2,256,128]{2,1,0:T(8,128)S(1)}, f32[2,256,128]{2,1,0:T(8,128)S(1)}, f32[2,256,128]{2,1,0:T(8,128)S(1)}, f32[2,8192]{1,0:T(2,128)S(1)}) custom-call(f32[2,256,128]{2,1,0:T(8,128)} %query_hbm.1, f32[2,256,128]{2,1,0:T(8,128)} %key_hbm.1, f32[2,256,128]{2,1,0:T(8,128)} %value_hbm.1, ...), custom_call_target="tpu_custom_call" | custom-call | tf_op jit(solution)/shard_map/spectral_exchange/pallas_call | solution.py:399
  27.6 1.1 %store.1 = (f32[2,256,128]{2,1,0:T(8,128)}, f32[2,256,128]{2,1,0:T(8,128)}, f32[2,256,128]{2,1,0:T(8,128)}, f32[2,256,128]{2,1,0:T(8,128)}, f32[2,8192]{1,0:T(2,128)}) custom-call(f32[2,256,128]{2,1,0:T(8,128)S(1)} %get-tuple-element.10.refs_0_, f32[2,256,128]{2,1,0:T(8,128)S(1)} %get-tuple-element.11.refs_1_, f32[2,256,128]{2,1,0:T(8,128)S(1)} %get-tuple-element.12.refs_2_, ...), custom_call_target="tpu_custom_call" | custom-call | tf_op jit(solution)/shard_map/store/pallas_call | solution.py:422

commit v6 on v5

--- a/solution.py
+++ b/solution.py
@@ -272,7 +272,7 @@
         rows = len(channels) * PART
         return pl.ds(pl.multiple_of(i * ROWS + channels[0] * PART, rows), rows)
 
-    def send(source, target, k, channels, partners):
+    def send(source, target, k, channels, partners, keep=True):
         for d in partners:
             pltpu.make_async_remote_copy(
                 src_ref=source.at[block(d, channels)],
@@ -282,7 +282,8 @@
                 device_id=(b, d),
                 device_id_type=MESH,
             ).start()
-        target[block(s, channels), :] = source[block(s, channels), :]
+        if keep:
+            target[block(s, channels), :] = source[block(s, channels), :]
 
     def settled(source, target, k, channels):
         rows = pl.ds(0, (PEERS - 1) * PART * len(channels))
@@ -321,11 +322,11 @@
         forward(mixed_got, mixed_spec, channels, tables)
         spread(inverse(mixed_spec, filter_spec, channels, False, tables, False), conv_send, channels)
         send(conv_send, conv_got, 2, channels, peers)
-    for channels in UP_CHUNKS:
-        settled(up_send, up_got, 1, channels).wait_recv()
-        forward(up_got, up_spec, channels, tables)
-        spread(inverse(filter_spec, up_spec, channels, True, tables, False), back_send, channels)
-        send(back_send, back_got, 3, channels, early_peers)
+    both = (0, 1)
+    settled(up_send, up_got, 1, both).wait_recv()
+    forward(up_got, up_spec, both, tables)
+    spread(inverse(filter_spec, up_spec, both, True, tables, False), back_send, both)
+    send(back_send, back_got, 3, both, early_peers[:2], False)
 
     result = inverse(mixed_spec, up_spec, (0, 1), True, tables, True)
     for half in range(2):
@@ -340,6 +341,7 @@
         device_id_type=MESH,
     )
     lag_copy.start()
+    send(back_send, back_got, 3, both, early_peers[2:])
 
     gain = skip[...]
     parts = [(bb, slice(h * 128, (h + 1) * 128), pl.ds(bb * 2 + h, 128, stride=4)) for bb in range(2) for h in range(2)]

time: 28.8 us -> 28.8 us (level)
  no operation moved by 1% of the time
where the time goes in v6:
time: 28.8 us; the launch traced here: 28.7 us
  Pallas kernels  28.1 us (98%)
  between operations  0.64 us (2%)
    pallas_call x1, Pallas kernels, per_device(): pl.pallas_call(main_kernel, out_shape=shapes, in_specs=[in_hbm] * len(ope...  27 us
    pallas_call x1, Pallas kernels, per_device(): pl.pallas_call(store_kernel, out_shape=shapes, in_specs=[pl.BlockSpec(mem...  1.06 us

profile of v6, /device:TPU:1, one launch (start us, length us, event | category | flops | bytes accessed | tf_op | source)
XLA Modules:
  0.0 28.7 jit_solution(206388492511094985)
XLA Ops:
  0.6 27.0 %spectral_exchange.1 = (f32[2,256,128]{2,1,0:T(8,128)S(1)}, f32[2,256,128]{2,1,0:T(8,128)S(1)}, f32[2,256,128]{2,1,0:T(8,128)S(1)}, f32[2,256,128]{2,1,0:T(8,128)S(1)}, f32[2,8192]{1,0:T(2,128)S(1)}) custom-call(f32[2,256,128]{2,1,0:T(8,128)} %query_hbm.1, f32[2,256,128]{2,1,0:T(8,128)} %key_hbm.1, f32[2,256,128]{2,1,0:T(8,128)} %value_hbm.1, ...), custom_call_target="tpu_custom_call" | custom-call | tf_op jit(solution)/shard_map/spectral_exchange/pallas_call | solution.py:401
  27.6 1.1 %store.1 = (f32[2,256,128]{2,1,0:T(8,128)}, f32[2,256,128]{2,1,0:T(8,128)}, f32[2,256,128]{2,1,0:T(8,128)}, f32[2,256,128]{2,1,0:T(8,128)}, f32[2,8192]{1,0:T(2,128)}) custom-call(f32[2,256,128]{2,1,0:T(8,128)S(1)} %get-tuple-element.10.refs_0_, f32[2,256,128]{2,1,0:T(8,128)S(1)} %get-tuple-element.11.refs_1_, f32[2,256,128]{2,1,0:T(8,128)S(1)} %get-tuple-element.12.refs_2_, ...), custom_call_target="tpu_custom_call" | custom-call | tf_op jit(solution)/shard_map/store/pallas_call | solution.py:424

commit v7 on v6

--- a/solution.py
+++ b/solution.py
@@ -224,6 +224,22 @@
     b = lax.axis_index("batch")
     s = lax.axis_index("seq")
 
+    places = (
+        [lax.rem(s // 16 + i, 4) * 16 for i in range(4)],
+        [lax.rem(s // 8 + i, 2) * 8 for i in range(2)],
+        [lax.rem(s // 2 + i, 4) * 2 for i in range(4)],
+    )
+    core = lax.rem(s, 2)
+    own = s - core
+    chips = [sum(place[i] for place, i in zip(places, shift)) for shift in SHIFTS]
+    peers = [chip + i for chip in chips for i in range(2)] + [own + 1 - core]
+    early = [jnp.where(own == 0, chips[0], 0)] + [jnp.where(chip == 0, chips[0], chip) for chip in chips[1:]]
+    early_peers = [chip + i for chip in early for i in range(2)] + [own + 1 - core]
+
+    barrier = pltpu.get_barrier_semaphore()
+    for d in peers[:24]:
+        pl.semaphore_signal(barrier, inc=1, device_id=(b, d), device_id_type=MESH)
+
     loads = [
         pltpu.make_async_copy(src, dst, load_sem.at[i])
         for i, (src, dst) in enumerate(
@@ -237,20 +253,7 @@
     for load in loads:
         load.start()
 
-    places = (
-        [lax.rem(s // 16 + i, 4) * 16 for i in range(4)],
-        [lax.rem(s // 8 + i, 2) * 8 for i in range(2)],
-        [lax.rem(s // 2 + i, 4) * 2 for i in range(4)],
-    )
-    core = lax.rem(s, 2)
-    own = s - core
-    chips = [sum(place[i] for place, i in zip(places, shift)) for shift in SHIFTS]
-    peers = [chip + i for chip in chips for i in range(2)] + [own + 1 - core]
-    early = [jnp.where(own == 0, chips[0], 0)] + [jnp.where(chip == 0, chips[0], chip) for chip in chips[1:]]
-    early_peers = [chip + i for chip in early for i in range(2)] + [own + 1 - core]
-
-    barrier = pltpu.get_barrier_semaphore()
-    for d in peers:
+    for d in peers[24:]:
         pl.semaphore_signal(barrier, inc=1, device_id=(b, d), device_id_type=MESH)
     pl.semaphore_signal(barrier, inc=1, device_id=(1 - b, s), device_id_type=MESH)
 

time: 28.8 us -> 28.9 us (level)
  no operation moved by 1% of the time
where the time goes in v7:
time: 28.9 us; the launch traced here: 28.7 us
  Pallas kernels  28.1 us (97%)
  between operations  0.64 us (2%)
    pallas_call x1, Pallas kernels, per_device(): pl.pallas_call(main_kernel, out_shape=shapes, in_specs=[in_hbm] * len(ope...  27 us
    pallas_call x1, Pallas kernels, per_device(): pl.pallas_call(store_kernel, out_shape=shapes, in_specs=[pl.BlockSpec(mem...  1.06 us

profile of v7, /device:TPU:1, one launch (start us, length us, event | category | flops | bytes accessed | tf_op | source)
XLA Modules:
  0.0 28.7 jit_solution(8585548118794627939)
XLA Ops:
  0.6 27.0 %spectral_exchange.1 = (f32[2,256,128]{2,1,0:T(8,128)S(1)}, f32[2,256,128]{2,1,0:T(8,128)S(1)}, f32[2,256,128]{2,1,0:T(8,128)S(1)}, f32[2,256,128]{2,1,0:T(8,128)S(1)}, f32[2,8192]{1,0:T(2,128)S(1)}) custom-call(f32[2,256,128]{2,1,0:T(8,128)} %query_hbm.1, f32[2,256,128]{2,1,0:T(8,128)} %key_hbm.1, f32[2,256,128]{2,1,0:T(8,128)} %value_hbm.1, ...), custom_call_target="tpu_custom_call" | custom-call | tf_op jit(solution)/shard_map/spectral_exchange/pallas_call | solution.py:404
  27.6 1.1 %store.1 = (f32[2,256,128]{2,1,0:T(8,128)}, f32[2,256,128]{2,1,0:T(8,128)}, f32[2,256,128]{2,1,0:T(8,128)}, f32[2,256,128]{2,1,0:T(8,128)}, f32[2,8192]{1,0:T(2,128)}) custom-call(f32[2,256,128]{2,1,0:T(8,128)S(1)} %get-tuple-element.10.refs_0_, f32[2,256,128]{2,1,0:T(8,128)S(1)} %get-tuple-element.11.refs_1_, f32[2,256,128]{2,1,0:T(8,128)S(1)} %get-tuple-element.12.refs_2_, ...), custom_call_target="tpu_custom_call" | custom-call | tf_op jit(solution)/shard_map/store/pallas_call | solution.py:427
